TPU v7x, 128 devices: a whole 4x4x4 slice. The times are simulated.
128 devices in a mesh: src: 4 (over x_lo, core), tgt: 32 (over y, x_hi, z).
Axes of the slice: x: 4 (x_hi: 2, x_lo: 2; x = x_hi * 2 + x_lo), y: 4, z: 4, core: 2. Of those that a mesh axis runs over, the one named last changes fastest.
Arguments:
- source_feat: bfloat16 [16384, 256], P(('src', 'tgt')), may hold values from -40 to 40
- target_feat: bfloat16 [57600, 256], P('tgt', 'src'), may hold values from -4 to 4
- proj: bfloat16 [256, 256], replicated, may hold values from -0.375 to 0.375
Outputs:
- flow: float32 [2, 16384], P(None, ('src', 'tgt'))
- matched: bfloat16 [16384, 256], P(('src', 'tgt'))
All inputs are finite; a program needn't handle non-finite values.
Results may differ from a plain program's by a relative error of at most 0.0075.
Values may be sent and summed in bfloat16 or wider, within the bound.
A program may use at most 256 MiB of HBM per device.

v0:
```python
import jax
import jax.numpy as jnp
from jax import lax
from jax.sharding import PartitionSpec as P

W_GRID = 320


def grid_coords(pos):
    return (
        (pos % W_GRID).astype(jnp.float32) / W_GRID,
        (pos // W_GRID).astype(jnp.float32) / W_GRID,
    )


def partial_block(queries, keys, key_start):
    width = queries.shape[1]
    scores = jnp.einsum("qc,kc->qk", queries, keys, preferred_element_type=jnp.float32) * width ** (
        -0.5
    )
    top = jnp.max(scores, axis=1)
    weights = jnp.exp(scores - top[:, None])
    total = jnp.sum(weights, axis=1)
    pos = key_start + jnp.arange(keys.shape[0], dtype=jnp.int32)
    grid_x, grid_y = grid_coords(pos)
    coord_sum = jnp.stack(
        [jnp.sum(weights * grid_x[None, :], axis=1), jnp.sum(weights * grid_y[None, :], axis=1)],
        axis=0,
    )
    feat_sum = jnp.dot(weights.astype(jnp.bfloat16), keys, preferred_element_type=jnp.float32)
    return (top, total, coord_sum, feat_sum)


def per_device(source_feat, target_feat, proj):
    width = proj.shape[1]
    own_rows = source_feat.shape[0]
    tgt_rows = target_feat.shape[0]
    strips = lax.axis_size("tgt")
    queries = jnp.dot(source_feat, proj, preferred_element_type=jnp.float32).astype(jnp.bfloat16)
    keys = jnp.dot(
        lax.all_gather(target_feat, "src", axis=1, tiled=True),
        proj,
        preferred_element_type=jnp.float32,
    ).astype(jnp.bfloat16)
    own_start = (lax.axis_index("src") * strips + lax.axis_index("tgt")) * own_rows
    strip = lax.all_gather(queries, "tgt", axis=0, tiled=True)
    strip_rows = strip.shape[0]
    block = min(256, strip_rows)
    key_start = lax.axis_index("tgt") * tgt_rows

    def one_block(qblock):
        return partial_block(qblock, keys, key_start)

    top, total, coord_sum, feat_sum = lax.map(
        one_block, strip.reshape(strip_rows // block, block, width)
    )
    top = top.reshape(strip_rows)
    total = total.reshape(strip_rows)
    coord_sum = jnp.moveaxis(coord_sum, 1, 0).reshape(2, strip_rows)
    feat_sum = feat_sum.reshape(strip_rows, width)
    largest = lax.pmax(top, "tgt")
    rescale = jnp.exp(top - largest)
    total, coord_sum, feat_sum = (
        lax.psum_scatter(total * rescale, "tgt", scatter_dimension=0, tiled=True),
        lax.psum_scatter(coord_sum * rescale[None, :], "tgt", scatter_dimension=1, tiled=True),
        lax.psum_scatter(feat_sum * rescale[:, None], "tgt", scatter_dimension=0, tiled=True),
    )
    own_pos = own_start + jnp.arange(own_rows, dtype=jnp.int32)
    own_x, own_y = grid_coords(own_pos)
    flow = jnp.stack([coord_sum[0] / total - own_x, coord_sum[1] / total - own_y], axis=0)
    matched = (feat_sum / total[:, None]).astype(jnp.bfloat16)
    return (flow, matched)


def solution(mesh):
    in_specs = (P(("src", "tgt"), None), P("tgt", "src"), P())
    out_specs = (P(None, ("src", "tgt")), P(("src", "tgt"), None))
    return jax.shard_map(
        per_device, mesh=mesh, in_specs=in_specs, out_specs=out_specs, check_vma=False
    )
```

profile of v0, /device:TPU:0, one launch (start us, length us, event | category | flops | bytes accessed | tf_op | source)
XLA Modules:
  0.0 709.4 jit_solution(2130675689377072865)
XLA Ops:
  8.1 1.6 convolution_convert_fusion.1
  9.8 10.0 %all_gather.7 = bf16[1800,256]{0,1:T(8,128)(2,1)S(1)} all-gather(bf16[1800,64]{0,1:T(8,128)(2,1)} %param.6), channel_id=1, replica_groups=mesh['src'=4,'tgt'=32] {'src'}, dimensions={1}, use_global_device_ids=true | all-gather | bytes 1152000 | tf_op jit(solution)/shard_map/all_gather | solution.py:41
  20.2 64.7 %all-gather.2.cloned.1.call-done = bf16[4096,256]{1,0:T(8,128)(2,1)} async-done(((bf16[128,256]{1,0:T(8,128)(2,1)}), bf16[4096,256]{1,0:T(8,128)(2,1)}) %all-gather.2.cloned.1.call-update) | async-done | bytes 2097168 | tf_op jit(solution)/shard_map/all_gather | solution.py:46
  84.9 61.6 %while.18 = (s32[]{:T(128)}, f32[16,256]{1,0:T(8,128)S(1)}, f32[16,256]{1,0:T(8,128)S(1)}, f32[16,2,256]{2,1,0:T(2,128)S(1)}, f32[16,256,256]{2,1,0:T(8,128)}, /...) while((s32[]{:T(128)}, f32[16,256]{1,0:T(8,128)S(1)}, ...), condition=%wide.region_5.6_spmd, body=%wide.region_0.5_spmd.sunk | while | flops 476497280 | bytes 7810293 | solution.py:54
  88.7 1.4 fusion.44
  92.6 1.4 fusion.44
  96.4 1.4 fusion.44
  100.3 1.4 fusion.44
  104.1 1.4 fusion.44
  108.0 1.4 fusion.44
  111.9 1.4 fusion.44
  115.7 1.4 fusion.44
  119.6 1.4 fusion.44
  123.4 1.4 fusion.44
  127.3 1.4 fusion.44
  131.1 1.4 fusion.44
  138.8 1.4 fusion.44
  142.7 1.4 fusion.44
  146.5 180.2 %pmax.7 = f32[4096]{0:T(1024)S(1)} all-reduce(f32[4096]{0:T(1024)S(1)} %bitcast.74), channel_id=1, replica_groups=mesh['src'=4,'tgt'=32] {'tgt'}, use_global_device_ids=true, to_apply=%region_6.7 | all-reduce | flops 4096 | bytes 32768 | tf_op jit(solution)/shard_map/pmax | solution.py:61
  326.8 2.1 copy.5
  329.0 3.9 bitcast_multiply_fusion
  334.8 176.2 %all-reduce = f32[4096]{0:T(1024)S(1)} all-reduce(f32[4096]{0:T(1024)S(1)} %get-tuple-element.134), channel_id=3, replica_groups=mesh['src'=4,'tgt'=32] {'tgt'}, use_global_device_ids=true, to_apply=%region_8.9.clone | all-reduce | flops 4096 | bytes 32768
  513.2 188.0 %reduce-scatter.5.cloned.1.call-done = f32[128,256]{1,0:T(8,128)} async-done(((f32[4096,256]{1,0:T(8,128)}), f32[128,256]{1,0:T(8,128)}) %reduce-scatter.5.cloned.1.call-update) | async-done | bytes 131088 | tf_op jit(solution)/shard_map/reduce_scatter | solution.py:66
  701.2 1.6 divide_convert_fusion
  (125 shorter events, 46.2 us)
Async XLA Ops:
  7.2 0.9 copy-start
  7.2 77.7 %all-gather.2.cloned.1.call-start = ((), (), s32[]{:S(2)}) async-start(), calls=%async_computation.2 | async-start | bytes 2162688 | tf_op jit(solution)/shard_map/all_gather | solution.py:46
  9.7 501.6 %reduce-scatter.7.cloned.1.call-start = ((), (), s32[]{:S(2)}) async-start(), calls=%async_computation.4 | async-start | bytes 2162688
  328.9 372.3 %reduce-scatter.5.cloned.1.call-start = ((), (), s32[]{:S(2)}) async-start(), calls=%async_computation.3 | async-start | bytes 4325376 | tf_op jit(solution)/shard_map/reduce_scatter | solution.py:66
  332.9 0.7 copy-start.1
Sparse Core Ops, SparseCore 0:
  11.7 73.2 all-gather.1
  329.0 182.2 reduce-scatter.6
  513.9 187.2 reduce-scatter.4
where the time goes:
time: 710 us; the launch traced here: 709 us
  blocking collectives  366 us (52%)
  waiting for transfers between devices  253 us (36%)
  matrix products  44.9 us (6%)
  other arithmetic  23.4 us (3%)
  between operations  14.5 us (2%)
    reduce_scatter x1, waiting for transfers between devices, per_device(): lax.psum_scatter(feat_sum * rescale[:, None], 'tgt', scatter_dimension=0,...  188 us
    pmax x1, blocking collectives, per_device(): largest = lax.pmax(top, 'tgt')  180 us
    unnamed x1, blocking collectives  176 us
    all_gather x1, waiting for transfers between devices, per_device(): strip = lax.all_gather(queries, 'tgt', axis=0, tiled=True)  64.7 us
    dot_general x16, matrix products, partial_block(): jnp.einsum('qc,kc->qk', queries, keys, preferred_element_type=jnp.float32)  22.6 us
    dot_general x16, matrix products, partial_block(): jnp.dot(weights.astype(jnp.bfloat16), keys, preferred_element_type=jnp.fl...  20.2 us
    reduce_sum x16, other arithmetic, partial_block(): jnp.sum(weights * grid_x[None, :], axis=1)  16.6 us
  transfers between devices with their start and end apart: 3, of which 3 were waited for; matrix products, arithmetic and copies ran while one was open for 1% of the time, Pallas kernels for 0%

commit v1 on v0

v1 whole, which is shorter than its diff:
```python
import jax
import jax.numpy as jnp
from jax import lax
from jax.experimental import pallas as pl
from jax.experimental.pallas import tpu as pltpu
from jax.sharding import PartitionSpec as P

MESH = pl.DeviceIdType.MESH
W_GRID = 320
C = 256
ROWS = 128
STRIP = 1800
HALF = 912
DUP = 2 * HALF - STRIP
KEYS = 4 * HALF
GROUP = 16
PAIRS = GROUP // 2
AUG = 16
F32 = jnp.float32
BF16 = jnp.bfloat16
NT = (((1,), (1,)), ((), ()))


def place():
    s, t = lax.axis_index("src"), lax.axis_index("tgt")
    return (t // 4 % 2) * 2 + s // 2, t // 8, t % 4, s % 2


def device(x, y, z, c):
    return ((x % 2) * 2 + c, (y * 2 + x // 2) * 4 + z)


def grid_of(pos):
    gy = jnp.floor((pos + 0.5) * (1.0 / W_GRID))
    return pos - gy * W_GRID, gy


def kernel(
    src_ref,
    tgt_ref,
    proj_ref,
    flow_ref,
    matched_ref,
    w_ref,
    pack,
    qbuf,
    keys,
    keys_t,
    s0,
    s1,
    m0,
    m1,
    stage,
    sstage,
    rbuf,
    rstat,
    p_send,
    p_recv,
    f_send,
    f_recv,
    q_send,
    q_recv,
    o_send,
    o_recv,
    t_send,
    t_recv,
):
    x, y, z, c = place()

    def yz(i, sign):
        j = (i + 1) % GROUP
        return device(x, (y + sign * (j // 4) + 4) % 4, (z + sign * (j % 4) + 4) % 4, c)

    sibling = device(x, y, z, 1 - c)

    barrier = pltpu.get_barrier_semaphore()

    def greet(i, carry):
        pl.semaphore_signal(barrier, inc=1, device_id=yz(i, 1), device_id_type=MESH)
        return carry

    lax.fori_loop(0, GROUP - 1, greet, 0)
    for k in range(1, 4):
        pl.semaphore_signal(
            barrier, inc=1, device_id=device((x + k) % 4, y, z, c), device_id_type=MESH
        )
    pl.semaphore_signal(barrier, inc=1, device_id=sibling, device_id_type=MESH)

    def slot_of(xx, cc):
        return (xx // 2) * 4 + (xx % 2) * 2 + cc

    own = slot_of(x, c)
    e_row = lax.broadcasted_iota(jnp.int32, (64, 128), 0)
    e_col = lax.broadcasted_iota(jnp.int32, (64, 128), 1)
    t32 = tgt_ref[...].astype(F32)
    packed = jnp.dot(
        t32[:HALF].astype(BF16), (e_row == e_col).astype(BF16), preferred_element_type=F32
    ) + jnp.dot(
        t32[STRIP - HALF :].astype(BF16),
        (e_row + 64 == e_col).astype(BF16),
        preferred_element_type=F32,
    )
    pack[own] = packed.astype(BF16)
    queries = jnp.dot(src_ref[...], proj_ref[...], preferred_element_type=F32).astype(BF16)
    own_q = pl.ds((GROUP - 1) * ROWS, ROWS)
    qbuf[own_q, :] = (queries.astype(F32) * (1.0 / 16.0)).astype(BF16)

    pl.semaphore_wait(barrier, GROUP - 1 + 4)

    def key_copy(k):
        return pltpu.make_async_remote_copy(
            src_ref=pack.at[own],
            dst_ref=pack.at[own],
            send_sem=p_send.at[k],
            recv_sem=p_recv.at[k],
            device_id=device((x + k) % 4, y, z, c),
            device_id_type=MESH,
        )

    def key_arrival(k):
        slot = slot_of((x - k + 4) % 4, c)
        return pltpu.make_async_remote_copy(
            src_ref=pack.at[slot],
            dst_ref=pack.at[slot],
            send_sem=p_send.at[k],
            recv_sem=p_recv.at[k],
            device_id=device((x - k + 4) % 4, y, z, c),
            device_id_type=MESH,
        )

    def forward(k):
        slot = slot_of((x - k + 4) % 4, c)
        return pltpu.make_async_remote_copy(
            src_ref=pack.at[slot],
            dst_ref=pack.at[slot],
            send_sem=f_send.at[k],
            recv_sem=f_recv.at[k],
            device_id=sibling,
            device_id_type=MESH,
        )

    def forward_arrival(k):
        slot = slot_of((x - k + 4) % 4, 1 - c)
        return pltpu.make_async_remote_copy(
            src_ref=pack.at[slot],
            dst_ref=pack.at[slot],
            send_sem=f_send.at[k],
            recv_sem=f_recv.at[k],
            device_id=sibling,
            device_id_type=MESH,
        )

    def query_copy(i):
        return pltpu.make_async_remote_copy(
            src_ref=qbuf.at[own_q],
            dst_ref=qbuf.at[pl.ds(pl.multiple_of(i * ROWS, ROWS), ROWS)],
            send_sem=q_send.at[i],
            recv_sem=q_recv.at[i],
            device_id=yz(i, -1),
            device_id_type=MESH,
        )

    def feat_copy(i):
        return pltpu.make_async_remote_copy(
            src_ref=stage.at[i],
            dst_ref=rbuf.at[i],
            send_sem=o_send.at[i],
            recv_sem=o_recv.at[i],
            device_id=yz(i, 1),
            device_id_type=MESH,
        )

    def stat_copy(i):
        return pltpu.make_async_remote_copy(
            src_ref=sstage.at[i],
            dst_ref=rstat.at[i],
            send_sem=t_send.at[i],
            recv_sem=t_recv.at[i],
            device_id=yz(i, 1),
            device_id_type=MESH,
        )

    for k in (1, 3, 2):
        key_copy(k).start()
    forward(0).start()

    def send_query(i, carry):
        query_copy(i).start()
        return carry

    lax.fori_loop(0, GROUP - 1, send_query, 0)

    w_ref[...] = jnp.zeros_like(w_ref)
    for d in range(4):
        rows = proj_ref[d * 64 : (d + 1) * 64, :]
        w_ref[d * 128 : d * 128 + 64, 0:C] = rows
        w_ref[d * 128 + 64 : (d + 1) * 128, C : 2 * C] = rows
    col = lax.broadcasted_iota(jnp.int32, (1, KEYS), 1)
    second = (col >= 2 * HALF).astype(jnp.int32)
    half = col - 2 * HALF * second
    right = (half >= HALF).astype(jnp.int32)
    valid = (half < HALF) | (half >= HALF + DUP)
    base = ((y * 2) * 4 + z) * STRIP
    pos = base + second * (4 * STRIP) + half - DUP * right
    kx, ky = grid_of(pos.astype(F32))
    kxh = jnp.floor(kx * (1.0 / 16.0))
    kxl = kx - 16.0 * kxh
    row = lax.broadcasted_iota(jnp.int32, (AUG, KEYS), 0)
    aug = jnp.where(
        row == 0, 1.0, jnp.where(row == 1, kxh, jnp.where(row == 2, kxl, jnp.where(row == 3, ky, 0.0)))
    )
    keys_t[C : C + AUG, :] = jnp.where(valid, aug, 0.0).astype(BF16)

    for k in (1, 3, 2):
        key_arrival(k).wait_recv()
        forward(k).start()
    for k in range(4):
        forward_arrival(k).wait_recv()

    for s in range(2):
        cat = jnp.concatenate([pack[4 * s + d] for d in range(4)], axis=1)
        a = jnp.dot(cat, w_ref[...], preferred_element_type=F32).astype(BF16)
        keys[2 * s * HALF : (2 * s + 1) * HALF, :] = a[:, :C]
        keys[(2 * s + 1) * HALF : (2 * s + 2) * HALF, :] = a[:, C:]
    i_row = lax.broadcasted_iota(jnp.int32, (C, C), 0)
    i_col = lax.broadcasted_iota(jnp.int32, (C, C), 1)
    kt = lax.dot_general(
        (i_row == i_col).astype(BF16), keys[...], NT, preferred_element_type=F32
    )
    keys_t[0:C, :] = jnp.where(valid, kt, 0.0).astype(BF16)

    def match(p, s_ref, m_ref):
        for i in (2 * p, 2 * p + 1):

            @pl.when(i < GROUP - 1)
            def _():
                query_copy(i).wait_recv()

        q = qbuf[pl.ds(pl.multiple_of(p * 2 * ROWS, 2 * ROWS), 2 * ROWS), :]
        s = lax.dot_general(keys[...], q, NT, preferred_element_type=F32)
        s_ref[...] = s
        m_ref[...] = jnp.max(s, axis=0, keepdims=True)

    def gather(p, s_ref, m_ref):
        m = m_ref[...]
        w = jnp.exp(s_ref[...] - m).astype(BF16)
        o = jnp.dot(keys_t[...], w, preferred_element_type=F32)
        srow = lax.broadcasted_iota(jnp.int32, (8, 2 * ROWS), 0)
        stat = jnp.where(srow == 4, m, o[C : C + 8, :])
        for e in range(2):
            i = 2 * p + e
            lanes = slice(e * ROWS, (e + 1) * ROWS)
            stage[i] = o[:C, lanes].astype(BF16)
            sstage[i] = stat[:, lanes]

            @pl.when(i < GROUP - 1)
            def _():
                feat_copy(i).start()
                stat_copy(i).start()

    match(0, s0, m0)

    def steps(j, carry):
        p = 2 * j
        match(p + 1, s1, m1)
        gather(p, s0, m0)
        match(p + 2, s0, m0)
        gather(p + 1, s1, m1)
        return carry

    lax.fori_loop(0, PAIRS // 2 - 1, steps, 0)
    match(PAIRS - 1, s1, m1)
    gather(PAIRS - 2, s0, m0)
    gather(PAIRS - 1, s1, m1)

    def settle(i, carry):
        query_copy(i).wait_send()
        feat_copy(i).wait_send()
        stat_copy(i).wait_send()
        feat_copy(i).wait_recv()
        stat_copy(i).wait_recv()
        return carry

    for k in range(1, 4):
        key_copy(k).wait_send()
    for k in range(4):
        forward(k).wait_send()
    lax.fori_loop(0, GROUP - 1, settle, 0)

    rstat[GROUP - 1] = sstage[GROUP - 1]
    top = rstat[0, 4:5, :]
    for i in range(1, GROUP):
        top = jnp.maximum(top, rstat[i, 4:5, :])
    total = jnp.zeros((8, ROWS), F32)
    feats = jnp.zeros((C, ROWS), F32)
    for i in range(GROUP):
        f = jnp.exp(rstat[i, 4:5, :] - top)
        part = rbuf[i] if i < GROUP - 1 else stage[i]
        total = total + rstat[i] * f
        feats = feats + part.astype(F32) * f
    inv = 1.0 / total[0:1]
    s_idx, t_idx = lax.axis_index("src"), lax.axis_index("tgt")
    lane = lax.broadcasted_iota(jnp.int32, (1, ROWS), 1)
    ox, oy = grid_of(((s_idx * 32 + t_idx) * ROWS + lane).astype(F32))
    cx = (total[1:2] * 16.0 + total[2:3]) * inv
    cy = total[3:4] * inv
    flow_ref[0:1, :] = (cx - ox) * (1.0 / W_GRID)
    flow_ref[1:2, :] = (cy - oy) * (1.0 / W_GRID)
    matched_ref[...] = (feats * inv).T.astype(BF16)


def per_device(source_feat, target_feat, proj):
    dma = pltpu.SemaphoreType.DMA
    vmem = pl.BlockSpec(memory_space=pltpu.VMEM)
    return pl.pallas_call(
        kernel,
        out_shape=(
            jax.ShapeDtypeStruct((2, ROWS), F32),
            jax.ShapeDtypeStruct((ROWS, C), BF16),
        ),
        in_specs=[vmem] * 3,
        out_specs=[vmem] * 2,
        scratch_shapes=[
            pltpu.VMEM((512, 512), BF16),
            pltpu.VMEM((8, HALF, 128), BF16),
            pltpu.VMEM((GROUP * ROWS, C), BF16),
            pltpu.VMEM((KEYS, C), BF16),
            pltpu.VMEM((C + AUG, KEYS), BF16),
            pltpu.VMEM((KEYS, 2 * ROWS), F32),
            pltpu.VMEM((KEYS, 2 * ROWS), F32),
            pltpu.VMEM((1, 2 * ROWS), F32),
            pltpu.VMEM((1, 2 * ROWS), F32),
            pltpu.VMEM((GROUP, C, ROWS), BF16),
            pltpu.VMEM((GROUP, 8, ROWS), F32),
            pltpu.VMEM((GROUP, C, ROWS), BF16),
            pltpu.VMEM((GROUP, 8, ROWS), F32),
            dma((4,)),
            dma((4,)),
            dma((4,)),
            dma((4,)),
            dma((GROUP,)),
            dma((GROUP,)),
            dma((GROUP,)),
            dma((GROUP,)),
            dma((GROUP,)),
            dma((GROUP,)),
        ],
        compiler_params=pltpu.CompilerParams(
            collective_id=0, has_side_effects=True, vmem_limit_bytes=50 << 20
        ),
        name="match_kernel",
    )(source_feat, target_feat, proj)


def solution(mesh):
    in_specs = (P(("src", "tgt"), None), P("tgt", "src"), P())
    out_specs = (P(None, ("src", "tgt")), P(("src", "tgt"), None))
    return jax.shard_map(
        per_device, mesh=mesh, in_specs=in_specs, out_specs=out_specs, check_vma=False
    )
```

time: 710 us -> 49.3 us (0.07)
  the two profiles are of different devices: /device:TPU:0 before, /device:TPU:1 now
where the time goes in v1:
time: 49.3 us; the launch traced here: 49.1 us
  Pallas kernels  46 us (93%)
  local copies, waits for them, and re-layouts  2.45 us (5%)
  between operations  0.67 us (1%)
    pallas_call x1, Pallas kernels, per_device(): pl.pallas_call(kernel, out_shape=(jax.ShapeDtypeStruct((2, ROWS), F32), j...  46 us
    unnamed x7, local copies, waits for them, and re-layouts  2.45 us

profile of v1, /device:TPU:1, one launch (start us, length us, event | category | flops | bytes accessed | tf_op | source)
XLA Modules:
  0.0 49.1 jit_solution(6419362495666027135)
XLA Ops:
  0.6 0.0 copy-start
  0.6 0.0 copy-start.1
  0.6 1.2 %copy.5.tgt_ref = bf16[1800,64]{1,0:T(8,128)(2,1)S(1)} copy(bf16[1800,64]{0,1:T(8,128)(2,1)} %param.4) | data formatting | bytes 460800 | tf_op args[1]
  1.9 0.0 copy-done
  1.9 0.0 copy-done.1
  1.9 46.0 %match_kernel.1 = (f32[2,128]{1,0:T(2,128)S(1)}, bf16[128,256]{1,0:T(8,128)(2,1)S(1)}) custom-call(bf16[128,256]{1,0:T(8,128)(2,1)S(1)} %copy-done.1, bf16[1800,64]{1,0:T(8,128)(2,1)S(1)} %copy.5.tgt_ref, bf16[256,256]{1,0:T(8,128)(2,1)S(1)} %copy-done), custom_call_target="tpu_custom_call" | custom-call | tf_op jit(solution)/shard_map/match_kernel/pallas_call | solution.py:315
  47.9 0.6 %copy.8 = f32[2,128]{1,0:T(2,128)} copy(f32[2,128]{1,0:T(2,128)S(1)} %get-tuple-element.4) | data formatting | bytes 2048
  48.5 0.6 %copy.9 = bf16[128,256]{1,0:T(8,128)(2,1)} copy(bf16[128,256]{1,0:T(8,128)(2,1)S(1)} %get-tuple-element.5) | data formatting | bytes 131072
Async XLA Ops:
  0.6 1.3 %copy-start = (bf16[256,256]{1,0:T(8,128)(2,1)S(1)}, bf16[256,256]{1,0:T(8,128)(2,1)}, u32[]{:S(2)}) copy-start(bf16[256,256]{1,0:T(8,128)(2,1)} %proj_ref.1) | copy-start | bytes 393220
  0.6 1.3 %copy-start.1 = (bf16[128,256]{1,0:T(8,128)(2,1)S(1)}, bf16[128,256]{1,0:T(8,128)(2,1)}, u32[]{:S(2)}) copy-start(bf16[128,256]{1,0:T(8,128)(2,1)} %src_ref.1) | copy-start | bytes 196612

commit v2 on v1

v2 whole, which is shorter than its diff:
```python
import jax
import jax.numpy as jnp
from jax import lax
from jax.experimental import pallas as pl
from jax.experimental.pallas import tpu as pltpu
from jax.sharding import PartitionSpec as P

MESH = pl.DeviceIdType.MESH
W_GRID = 320
C = 256
ROWS = 128
STRIP = 1800
GROUP = 16
PAIRS = GROUP // 2
CROWS = 64
HCH = CROWS // 2
AUG = 16
F32 = jnp.float32
BF16 = jnp.bfloat16
NT = (((1,), (1,)), ((), ()))
TN = (((0,), (0,)), ((), ()))
OFFSETS = (
    (1, 2), (2, 1), (3, 2), (2, 3), (2, 2), (1, 1), (3, 3), (1, 3),
    (3, 1), (0, 2), (2, 0), (0, 1), (1, 0), (0, 3), (3, 0), (0, 0),
)


def table(which, half):
    return sum(OFFSETS[8 * half + k][which] * 4**k for k in range(8))


def offset(which, i):
    tab = jnp.where(i < 8, table(which, 0), table(which, 1))
    return lax.shift_right_logical(tab, 2 * (i % 8)) % 4


def place():
    s, t = lax.axis_index("src"), lax.axis_index("tgt")
    return (t // 4 % 2) * 2 + s // 2, t // 8, t % 4, s % 2


def device(x, y, z, c):
    return ((x % 2) * 2 + c, (y * 2 + x // 2) * 4 + z)


def grid_of(pos):
    gy = jnp.floor((pos + 0.5) * (1.0 / W_GRID))
    return pos - gy * W_GRID, gy


def kernel(
    src_ref,
    tgt_ref,
    proj_ref,
    flow_ref,
    matched_ref,
    chans,
    qbuf,
    keys,
    keys_t,
    scores,
    top_ref,
    stage,
    sstage,
    rbuf,
    rstat,
    p_send,
    p_recv,
    f_send,
    f_recv,
    q_send,
    q_recv,
    o_send,
    o_recv,
    t_send,
    t_recv,
):
    x, y, z, c = place()

    def yz(i, sign):
        dy, dz = offset(0, i), offset(1, i)
        return device(x, (y + sign * dy + 4) % 4, (z + sign * dz + 4) % 4, c)

    sibling = device(x, y, z, 1 - c)

    barrier = pltpu.get_barrier_semaphore()

    def greet(i, carry):
        pl.semaphore_signal(barrier, inc=1, device_id=yz(i, 1), device_id_type=MESH)
        return carry

    lax.fori_loop(0, GROUP - 1, greet, 0)
    left, right = device((x + 3) % 4, y, z, c), device((x + 1) % 4, y, z, c)
    for other in (left, right):
        pl.semaphore_signal(barrier, inc=1, device_id=other, device_id_type=MESH)
    pl.semaphore_signal(barrier, inc=1, device_id=sibling, device_id_type=MESH)

    def piece(dx, cc, start, size):
        xx = (x + dx) % 4
        first = ((xx % 2) * 2 + cc) * CROWS + start
        return chans.at[xx // 2, pl.ds(pl.multiple_of(first, HCH), size)]

    piece(0, c, 0, CROWS)[...] = tgt_ref[...]
    queries = jnp.dot(src_ref[...], proj_ref[...], preferred_element_type=F32).astype(BF16)
    own_q = pl.ds((GROUP - 1) * ROWS, ROWS)
    qbuf[own_q, :] = (queries.astype(F32) * (1.0 / 16.0)).astype(BF16)

    pl.semaphore_wait(barrier, GROUP - 1 + 3)

    ring = ((1, 0, 0), (-1, 0, 1), (1, 0, 1), (-1, 0, 0), (1, -1, 0), (-1, 1, 1))

    def ring_copy(k, arrival):
        step, owner, h = ring[k]
        ref = piece(owner - step * arrival + 4, c, h * HCH, HCH)
        return pltpu.make_async_remote_copy(
            src_ref=ref,
            dst_ref=ref,
            send_sem=p_send.at[k],
            recv_sem=p_recv.at[k],
            device_id=right if step == 1 else left,
            device_id_type=MESH,
        )

    def core_copy(k, arrival):
        cc = 1 - c if arrival else c
        if k == len(ring):
            ref = piece(0, cc, 0, CROWS)
        else:
            step, owner, h = ring[k]
            ref = piece(owner - step + 4, cc, h * HCH, HCH)
        return pltpu.make_async_remote_copy(
            src_ref=ref,
            dst_ref=ref,
            send_sem=f_send.at[k],
            recv_sem=f_recv.at[k],
            device_id=sibling,
            device_id_type=MESH,
        )

    def query_copy(i):
        return pltpu.make_async_remote_copy(
            src_ref=qbuf.at[own_q],
            dst_ref=qbuf.at[pl.ds(pl.multiple_of(i * ROWS, ROWS), ROWS)],
            send_sem=q_send.at[i],
            recv_sem=q_recv.at[i],
            device_id=yz(i, -1),
            device_id_type=MESH,
        )

    def feat_copy(i):
        return pltpu.make_async_remote_copy(
            src_ref=stage.at[i],
            dst_ref=rbuf.at[i],
            send_sem=o_send.at[i],
            recv_sem=o_recv.at[i],
            device_id=yz(i, 1),
            device_id_type=MESH,
        )

    def stat_copy(i):
        return pltpu.make_async_remote_copy(
            src_ref=sstage.at[i],
            dst_ref=rstat.at[i],
            send_sem=t_send.at[i],
            recv_sem=t_recv.at[i],
            device_id=yz(i, 1),
            device_id_type=MESH,
        )

    for k in range(4):
        ring_copy(k, False).start()
    core_copy(6, False).start()

    def send_query(i, carry):
        query_copy(i).start()
        return carry

    lax.fori_loop(0, GROUP - 1, send_query, 0)

    mine = x // 2
    col = lax.broadcasted_iota(jnp.int32, (1, STRIP), 1)
    row = lax.broadcasted_iota(jnp.int32, (AUG, STRIP), 0)
    for e in range(2):
        strip = mine if e == 0 else 1 - mine
        base = ((y * 2 + strip) * 4 + z) * STRIP
        kx, ky = grid_of((base + col).astype(F32))
        kxh = jnp.floor(kx * (1.0 / 16.0))
        kxl = kx - 16.0 * kxh
        aug = jnp.where(
            row == 0,
            1.0,
            jnp.where(row == 1, kxh, jnp.where(row == 2, kxl, jnp.where(row == 3, ky, 0.0))),
        )
        keys_t[e, C : C + AUG, :] = aug.astype(BF16)

    def project(e):
        block = chans[mine if e == 0 else 1 - mine]
        keys[e] = lax.dot_general(block, proj_ref[...], TN, preferred_element_type=F32).astype(BF16)
        keys_t[e, 0:C, :] = lax.dot_general(
            proj_ref[...], block, TN, preferred_element_type=F32
        ).astype(BF16)

    for k in range(2):
        ring_copy(k, True).wait_recv()
        ring_copy(k + 4, False).start()
        core_copy(k, False).start()
    for k in range(2, 4):
        ring_copy(k, True).wait_recv()
        core_copy(k, False).start()
    for k in (6, 0, 1, 2, 3):
        core_copy(k, True).wait_recv()
    project(0)
    for k in range(4, 6):
        ring_copy(k, True).wait_recv()
        core_copy(k, False).start()
    for k in range(4, 6):
        core_copy(k, True).wait_recv()
    project(1)

    def pair(p, carry):
        def match(_, inner):
            for i in (2 * p, 2 * p + 1):

                @pl.when(i < GROUP - 1)
                def _():
                    query_copy(i).wait_recv()

            q = qbuf[pl.ds(pl.multiple_of(p * 2 * ROWS, 2 * ROWS), 2 * ROWS), :]
            tops = []
            for e in range(2):
                s = lax.dot_general(keys[e], q, NT, preferred_element_type=F32)
                scores[e] = s
                tops.append(jnp.max(s, axis=0, keepdims=True))
            top_ref[...] = jnp.maximum(tops[0], tops[1])
            return inner

        def gather(_, inner):
            m = top_ref[...]
            o = jnp.zeros((C + AUG, 2 * ROWS), F32)
            for e in range(2):
                w = jnp.exp(scores[e] - m).astype(BF16)
                o = o + jnp.dot(keys_t[e], w, preferred_element_type=F32)
            srow = lax.broadcasted_iota(jnp.int32, (8, 2 * ROWS), 0)
            stat = jnp.where(srow == 4, m, o[C : C + 8, :])
            for e in range(2):
                i = 2 * p + e
                lanes = slice(e * ROWS, (e + 1) * ROWS)
                stage[i] = o[:C, lanes].astype(BF16)
                sstage[i] = stat[:, lanes]

                @pl.when(i < GROUP - 1)
                def _():
                    feat_copy(i).start()
                    stat_copy(i).start()

            return inner

        lax.fori_loop(p, p + 1, match, 0)
        lax.fori_loop(p, p + 1, gather, 0)
        return carry

    lax.fori_loop(0, PAIRS, pair, 0)

    def settle(i, carry):
        query_copy(i).wait_send()
        feat_copy(i).wait_send()
        stat_copy(i).wait_send()
        feat_copy(i).wait_recv()
        stat_copy(i).wait_recv()
        return carry

    for k in range(6):
        ring_copy(k, False).wait_send()
    for k in range(7):
        core_copy(k, False).wait_send()
    lax.fori_loop(0, GROUP - 1, settle, 0)

    rstat[GROUP - 1] = sstage[GROUP - 1]
    top = rstat[0, 4:5, :]
    for i in range(1, GROUP):
        top = jnp.maximum(top, rstat[i, 4:5, :])
    total = jnp.zeros((8, ROWS), F32)
    feats = jnp.zeros((C, ROWS), F32)
    for i in range(GROUP):
        f = jnp.exp(rstat[i, 4:5, :] - top)
        part = rbuf[i] if i < GROUP - 1 else stage[i]
        total = total + rstat[i] * f
        feats = feats + part.astype(F32) * f
    inv = 1.0 / total[0:1]
    s_idx, t_idx = lax.axis_index("src"), lax.axis_index("tgt")
    lane = lax.broadcasted_iota(jnp.int32, (1, ROWS), 1)
    ox, oy = grid_of(((s_idx * 32 + t_idx) * ROWS + lane).astype(F32))
    cx = (total[1:2] * 16.0 + total[2:3]) * inv
    cy = total[3:4] * inv
    flow_ref[0:1, :] = (cx - ox) * (1.0 / W_GRID)
    flow_ref[1:2, :] = (cy - oy) * (1.0 / W_GRID)
    matched_ref[...] = (feats * inv).T.astype(BF16)


def per_device(source_feat, target_feat, proj):
    dma = pltpu.SemaphoreType.DMA
    vmem = pl.BlockSpec(memory_space=pltpu.VMEM)
    return pl.pallas_call(
        kernel,
        out_shape=(
            jax.ShapeDtypeStruct((2, ROWS), F32),
            jax.ShapeDtypeStruct((ROWS, C), BF16),
        ),
        in_specs=[vmem] * 3,
        out_specs=[vmem] * 2,
        scratch_shapes=[
            pltpu.VMEM((2, C, STRIP), BF16),
            pltpu.VMEM((GROUP * ROWS, C), BF16),
            pltpu.VMEM((2, STRIP, C), BF16),
            pltpu.VMEM((2, C + AUG, STRIP), BF16),
            pltpu.VMEM((2, STRIP, 2 * ROWS), F32),
            pltpu.VMEM((1, 2 * ROWS), F32),
            pltpu.VMEM((GROUP, C, ROWS), BF16),
            pltpu.VMEM((GROUP, 8, ROWS), F32),
            pltpu.VMEM((GROUP, C, ROWS), BF16),
            pltpu.VMEM((GROUP, 8, ROWS), F32),
            dma((6,)),
            dma((6,)),
            dma((7,)),
            dma((7,)),
            dma((GROUP,)),
            dma((GROUP,)),
            dma((GROUP,)),
            dma((GROUP,)),
            dma((GROUP,)),
            dma((GROUP,)),
        ],
        compiler_params=pltpu.CompilerParams(
            collective_id=0, has_side_effects=True, vmem_limit_bytes=50 << 20
        ),
        name="match_kernel",
    )(source_feat, target_feat.T, proj)


def solution(mesh):
    in_specs = (P(("src", "tgt"), None), P("tgt", "src"), P())
    out_specs = (P(None, ("src", "tgt")), P(("src", "tgt"), None))
    return jax.shard_map(
        per_device, mesh=mesh, in_specs=in_specs, out_specs=out_specs, check_vma=False
    )
```

time: 49.3 us -> 43.3 us (0.88)
  Pallas kernels: 46 us -> 38.6 us
  local copies, waits for them, and re-layouts: 2.45 us -> 3.87 us
    pallas_call x1, Pallas kernels: 46 us -> 38.6 us  [per_device(): pl.pallas_call(kernel, out_shape=(jax.ShapeDtypeStruct((2, ROWS), F32), j...]
    unnamed x7 -> x8, local copies, waits for them, and re-layouts: 2.45 us -> 3.87 us
where the time goes in v2:
time: 43.3 us; the launch traced here: 43.1 us
  Pallas kernels  38.6 us (89%)
  local copies, waits for them, and re-layouts  3.87 us (9%)
  between operations  0.65 us (2%)
    pallas_call x1, Pallas kernels, per_device(): pl.pallas_call(kernel, out_shape=(jax.ShapeDtypeStruct((2, ROWS), F32), j...  38.6 us
    unnamed x8, local copies, waits for them, and re-layouts  3.87 us

profile of v2, /device:TPU:1, one launch (start us, length us, event | category | flops | bytes accessed | tf_op | source)
XLA Modules:
  0.0 43.1 jit_solution(4108423049544935026)
XLA Ops:
  0.6 0.0 copy-start
  0.6 0.9 %copy-done = bf16[1800,64]{0,1:T(8,128)(2,1)S(1)} copy-done((bf16[1800,64]{0,1:T(8,128)(2,1)S(1)}, bf16[1800,64]{0,1:T(8,128)(2,1)}, u32[]{:S(2)}) %copy-start) | copy-done | bytes 230424
  1.6 0.0 copy-start.1
  1.6 0.9 %copy-done.1 = bf16[256,256]{1,0:T(8,128)(2,1)S(1)} copy-done((bf16[256,256]{1,0:T(8,128)(2,1)S(1)}, bf16[256,256]{1,0:T(8,128)(2,1)}, u32[]{:S(2)}) %copy-start.1) | copy-done | bytes 131096
  2.5 0.0 copy-start.2
  2.5 0.8 %copy-done.2 = bf16[128,256]{1,0:T(8,128)(2,1)S(1)} copy-done((bf16[128,256]{1,0:T(8,128)(2,1)S(1)}, bf16[128,256]{1,0:T(8,128)(2,1)}, u32[]{:S(2)}) %copy-start.2) | copy-done | bytes 65560
  3.3 38.6 %match_kernel.1 = (f32[2,128]{1,0:T(2,128)S(1)}, bf16[128,256]{1,0:T(8,128)(2,1)S(1)}) custom-call(bf16[128,256]{1,0:T(8,128)(2,1)S(1)} %copy-done.2, bf16[64,1800]{1,0:T(8,128)(2,1)S(1)} %bitcast.1, bf16[256,256]{1,0:T(8,128)(2,1)S(1)} %copy-done.1), custom_call_target="tpu_custom_call" | custom-call | tf_op jit(solution)/shard_map/match_kernel/pallas_call | solution.py:303
  41.9 0.6 %copy.7 = f32[2,128]{1,0:T(2,128)} copy(f32[2,128]{1,0:T(2,128)S(1)} %get-tuple-element.4) | data formatting | bytes 2048
  42.5 0.6 %copy.8 = bf16[128,256]{1,0:T(8,128)(2,1)} copy(bf16[128,256]{1,0:T(8,128)(2,1)S(1)} %get-tuple-element.5) | data formatting | bytes 131072
Async XLA Ops:
  0.6 0.9 %copy-start = (bf16[1800,64]{0,1:T(8,128)(2,1)S(1)}, bf16[1800,64]{0,1:T(8,128)(2,1)}, u32[]{:S(2)}) copy-start(bf16[1800,64]{0,1:T(8,128)(2,1)} %param.4) | copy-start | bytes 691204
  1.6 0.9 %copy-start.1 = (bf16[256,256]{1,0:T(8,128)(2,1)S(1)}, bf16[256,256]{1,0:T(8,128)(2,1)}, u32[]{:S(2)}) copy-start(bf16[256,256]{1,0:T(8,128)(2,1)} %proj_ref.1) | copy-start | bytes 393220
  2.5 0.8 %copy-start.2 = (bf16[128,256]{1,0:T(8,128)(2,1)S(1)}, bf16[128,256]{1,0:T(8,128)(2,1)}, u32[]{:S(2)}) copy-start(bf16[128,256]{1,0:T(8,128)(2,1)} %src_ref.1) | copy-start | bytes 196612

commit v3 on v2

v3 whole, which is shorter than its diff:
```python
import jax
import jax.numpy as jnp
from jax import lax
from jax.experimental import pallas as pl
from jax.experimental.pallas import tpu as pltpu
from jax.sharding import PartitionSpec as P

MESH = pl.DeviceIdType.MESH
W_GRID = 320
C = 256
ROWS = 128
STRIP = 1800
CROWS = 64
HCH = CROWS // 2
N = 4
GROUP = N * N
AUG = 16
TOP = 4
F32 = jnp.float32
BF16 = jnp.bfloat16
NT = (((1,), (1,)), ((), ()))
TN = (((0,), (0,)), ((), ()))
RING = ((1, 0, 0), (-1, 0, 1), (1, 0, 1), (-1, 0, 0), (1, -1, 0), (-1, 1, 1))


def place():
    s, t = lax.axis_index("src"), lax.axis_index("tgt")
    return (t // 4 % 2) * 2 + s // 2, t // 8, t % 4, s % 2


def device(x, y, z, c):
    return ((x % 2) * 2 + c, (y * 2 + x // 2) * 4 + z)


def grid_of(pos):
    gy = jnp.floor((pos + 0.5) * (1.0 / W_GRID))
    return pos - gy * W_GRID, gy


def merge(feats, stats):
    top = stats[0][TOP : TOP + 1]
    for stat in stats[1:]:
        top = jnp.maximum(top, stat[TOP : TOP + 1])
    feat_sum = stat_sum = None
    for feat, stat in zip(feats, stats):
        f = jnp.exp(stat[TOP : TOP + 1] - top)
        feat, stat = feat.astype(F32) * f, stat * f
        feat_sum = feat if feat_sum is None else feat_sum + feat
        stat_sum = stat if stat_sum is None else stat_sum + stat
    return top, feat_sum, stat_sum


def kernel(
    src_hbm,
    tgt_hbm,
    proj_hbm,
    flow_ref,
    matched_ref,
    src_ref,
    proj_ref,
    chans,
    qbuf,
    keys,
    keys_t,
    scores,
    top_ref,
    stage,
    sstage,
    inbox,
    sinbox,
    rout,
    srout,
    rin,
    srin,
    in_sems,
    p_send,
    p_recv,
    f_send,
    f_recv,
    q1_send,
    q1_recv,
    q2_send,
    q2_recv,
    o_send,
    o_recv,
    t_send,
    t_recv,
    ro_send,
    ro_recv,
    rt_send,
    rt_recv,
):
    x, y, z, c = place()
    a, b = z + c * (y - z), y + c * (z - y)

    def peer(da, db):
        aa, bb = (a + da) % N, (b + db) % N
        return device(x, bb + c * (aa - bb), aa + c * (bb - aa), c)

    sibling = device(x, y, z, 1 - c)
    left, right = device((x + 3) % N, y, z, c), device((x + 1) % N, y, z, c)

    def piece(dx, cc, start, size):
        xx = (x + dx) % N
        first = ((xx % 2) * 2 + cc) * CROWS + start
        return chans.at[xx // 2, pl.ds(pl.multiple_of(first, HCH), size)]

    loads = (
        pltpu.make_async_copy(tgt_hbm, piece(0, c, 0, CROWS), in_sems.at[0]),
        pltpu.make_async_copy(proj_hbm, proj_ref, in_sems.at[1]),
        pltpu.make_async_copy(src_hbm, src_ref, in_sems.at[2]),
    )
    barrier = pltpu.get_barrier_semaphore()
    for other in (left, right, sibling):
        pl.semaphore_signal(barrier, inc=1, device_id=other, device_id_type=MESH)
    for k in range(1, N):
        pl.semaphore_signal(barrier, inc=1, device_id=peer(k, 0), device_id_type=MESH)
        pl.semaphore_signal(barrier, inc=1, device_id=peer(0, k), device_id_type=MESH)
    for load in loads:
        load.start()
    pl.semaphore_wait(barrier, 3 + 2 * (N - 1))

    def remote(src, dst, send_sem, recv_sem, other):
        return pltpu.make_async_remote_copy(
            src_ref=src,
            dst_ref=dst,
            send_sem=send_sem,
            recv_sem=recv_sem,
            device_id=other,
            device_id_type=MESH,
        )

    def ring_copy(k, arrival):
        step, owner, h = RING[k]
        ref = piece(owner - step * arrival + N, c, h * HCH, HCH)
        fresh = owner == 0 and not arrival
        src = tgt_hbm.at[pl.ds(h * HCH, HCH)] if fresh else ref
        return remote(src, ref, p_send.at[k], p_recv.at[k], right if step == 1 else left)

    def core_copy(k, arrival):
        cc = 1 - c if arrival else c
        if k == len(RING):
            ref = piece(0, cc, 0, CROWS)
        else:
            step, owner, h = RING[k]
            ref = piece(owner - step + N, cc, h * HCH, HCH)
        src = tgt_hbm if k == len(RING) and not arrival else ref
        return remote(src, ref, f_send.at[k], f_recv.at[k], sibling)

    def q_block(k, arrival):
        ref = qbuf.at[b * N + (a + (N - k if arrival else 0)) % N]
        return remote(ref, ref, q1_send.at[k], q1_recv.at[k], peer(k, 0))

    def q_row(k, arrival):
        row = (b + (N - k if arrival else 0)) % N
        ref = qbuf.at[pl.ds(row * N, N)]
        return remote(ref, ref, q2_send.at[k], q2_recv.at[k], peer(0, k))

    def feat_copy(r, j):
        i = r * N + j
        return remote(stage.at[i], inbox.at[i], o_send.at[i], o_recv.at[i], peer(j, 0))

    def stat_copy(r, j):
        i = r * N + j
        return remote(sstage.at[i], sinbox.at[i], t_send.at[i], t_recv.at[i], peer(j, 0))

    def relay_feat(r):
        return remote(rout.at[r], rin.at[r], ro_send.at[r], ro_recv.at[r], peer(0, r))

    def relay_stat(r):
        return remote(srout.at[r], srin.at[r], rt_send.at[r], rt_recv.at[r], peer(0, r))

    for k in range(4):
        ring_copy(k, False).start()
    core_copy(6, False).start()

    for load in loads:
        load.wait()
    queries = jnp.dot(src_ref[...], proj_ref[...], preferred_element_type=F32).astype(BF16)
    qbuf[b * N + a] = (queries.astype(F32) * (1.0 / 16.0)).astype(BF16)
    for k in range(1, N):
        q_block(k, False).start()

    mine = x // 2
    col = lax.broadcasted_iota(jnp.int32, (1, STRIP), 1)
    row = lax.broadcasted_iota(jnp.int32, (AUG, STRIP), 0)
    for e in range(2):
        strip = mine if e == 0 else 1 - mine
        base = ((y * 2 + strip) * 4 + z) * STRIP
        kx, ky = grid_of((base + col).astype(F32))
        kxh = jnp.floor(kx * (1.0 / 16.0))
        kxl = kx - 16.0 * kxh
        aug = jnp.where(
            row == 0,
            1.0,
            jnp.where(row == 1, kxh, jnp.where(row == 2, kxl, jnp.where(row == 3, ky, 0.0))),
        )
        keys_t[e, C : C + AUG, :] = aug.astype(BF16)

    def project(e):
        block = chans[mine if e == 0 else 1 - mine]
        keys[e] = lax.dot_general(block, proj_ref[...], TN, preferred_element_type=F32).astype(BF16)
        keys_t[e, 0:C, :] = lax.dot_general(
            proj_ref[...], block, TN, preferred_element_type=F32
        ).astype(BF16)

    for k in range(2):
        ring_copy(k, True).wait_recv()
        ring_copy(k + 4, False).start()
        core_copy(k, False).start()
    for k in range(1, N):
        q_block(k, True).wait_recv()
    for k in (3, 2, 1):
        q_row(k, False).start()
    for k in range(2, 4):
        ring_copy(k, True).wait_recv()
        core_copy(k, False).start()
    for k in (6, 0, 1, 2, 3):
        core_copy(k, True).wait_recv()
    project(0)
    for k in range(4, 6):
        ring_copy(k, True).wait_recv()
        core_copy(k, False).start()
    for k in range(4, 6):
        core_copy(k, True).wait_recv()
    project(1)

    def relay(r):
        for j in range(1, N):
            feat_copy(r, j).wait_recv()
            stat_copy(r, j).wait_recv()
        i = r * N
        top, feat, stat = merge(
            [stage[i]] + [inbox[i + j] for j in range(1, N)],
            [sstage[i]] + [sinbox[i + j] for j in range(1, N)],
        )
        srow = lax.broadcasted_iota(jnp.int32, (8, ROWS), 0)
        rout[r] = feat.astype(BF16)
        srout[r] = jnp.where(srow == TOP, top, stat)
        relay_feat(r).start()
        relay_stat(r).start()

    def turn(t, carry):
        r = (t // 2 + 1) % N
        js = (2 * (t % 2) + 1, (2 * (t % 2) + 2) % N)

        @pl.when((t % 2 == 0) & (t < 6))
        def _():
            q_row(N - r, True).wait_recv()

        def match(_, inner):
            base = ((b + r) % N) * N
            q = jnp.concatenate([qbuf[base + (a + j) % N] for j in js], axis=0)
            tops = []
            for e in range(2):
                s = lax.dot_general(keys[e], q, NT, preferred_element_type=F32)
                scores[e] = s
                tops.append(jnp.max(s, axis=0, keepdims=True))
            top_ref[...] = jnp.maximum(tops[0], tops[1])
            return inner

        def gather(_, inner):
            m = top_ref[...]
            o = jnp.zeros((C + AUG, 2 * ROWS), F32)
            for e in range(2):
                w = jnp.exp(scores[e] - m).astype(BF16)
                o = o + jnp.dot(keys_t[e], w, preferred_element_type=F32)
            srow = lax.broadcasted_iota(jnp.int32, (8, 2 * ROWS), 0)
            stat = jnp.where(srow == TOP, m, o[C : C + 8, :])
            for e, j in enumerate(js):
                lanes = slice(e * ROWS, (e + 1) * ROWS)
                stage[r * N + j] = o[:C, lanes].astype(BF16)
                sstage[r * N + j] = stat[:, lanes]

                @pl.when(j > 0)
                def _():
                    feat_copy(r, j).start()
                    stat_copy(r, j).start()

            return inner

        lax.fori_loop(t, t + 1, match, 0)
        lax.fori_loop(t, t + 1, gather, 0)

        @pl.when((t % 2 == 1) & (t > 1))
        def _():
            relay((t - 1) // 2)

        return carry

    lax.fori_loop(0, 2 * N, turn, 0)

    for j in range(1, N):
        feat_copy(0, j).wait_recv()
        stat_copy(0, j).wait_recv()
    for r in range(1, N):
        relay_feat(r).wait_recv()
        relay_stat(r).wait_recv()
    _, feats, total = merge(
        [stage[0]] + [inbox[j] for j in range(1, N)] + [rin[r] for r in range(1, N)],
        [sstage[0]] + [sinbox[j] for j in range(1, N)] + [srin[r] for r in range(1, N)],
    )
    inv = 1.0 / total[0:1]
    s_idx, t_idx = lax.axis_index("src"), lax.axis_index("tgt")
    lane = lax.broadcasted_iota(jnp.int32, (1, ROWS), 1)
    ox, oy = grid_of(((s_idx * 32 + t_idx) * ROWS + lane).astype(F32))
    cx = (total[1:2] * 16.0 + total[2:3]) * inv
    cy = total[3:4] * inv
    flow_ref[0:1, :] = (cx - ox) * (1.0 / W_GRID)
    flow_ref[1:2, :] = (cy - oy) * (1.0 / W_GRID)
    matched_ref[...] = (feats * inv).T.astype(BF16)

    for k in range(6):
        ring_copy(k, False).wait_send()
    for k in range(7):
        core_copy(k, False).wait_send()
    for k in range(1, N):
        q_block(k, False).wait_send()
        q_row(k, False).wait_send()
        relay_feat(k).wait_send()
        relay_stat(k).wait_send()

    def settle(i, carry):
        r, j = i // (N - 1), i % (N - 1) + 1
        feat_copy(r, j).wait_send()
        stat_copy(r, j).wait_send()
        return carry

    lax.fori_loop(0, N * (N - 1), settle, 0)


def per_device(source_feat, target_feat, proj):
    dma = pltpu.SemaphoreType.DMA
    vmem = pl.BlockSpec(memory_space=pltpu.VMEM)
    args = (source_feat, target_feat.T, proj)
    return pl.pallas_call(
        kernel,
        out_shape=(
            jax.ShapeDtypeStruct((2, ROWS), F32),
            jax.ShapeDtypeStruct((ROWS, C), BF16),
        ),
        in_specs=[pl.BlockSpec(memory_space=pltpu.HBM)] * 3,
        out_specs=[vmem] * 2,
        scratch_shapes=[
            pltpu.VMEM((ROWS, C), BF16),
            pltpu.VMEM((C, C), BF16),
            pltpu.VMEM((2, C, STRIP), BF16),
            pltpu.VMEM((GROUP, ROWS, C), BF16),
            pltpu.VMEM((2, STRIP, C), BF16),
            pltpu.VMEM((2, C + AUG, STRIP), BF16),
            pltpu.VMEM((2, STRIP, 2 * ROWS), F32),
            pltpu.VMEM((1, 2 * ROWS), F32),
            pltpu.VMEM((GROUP, C, ROWS), BF16),
            pltpu.VMEM((GROUP, 8, ROWS), F32),
            pltpu.VMEM((GROUP, C, ROWS), BF16),
            pltpu.VMEM((GROUP, 8, ROWS), F32),
            pltpu.VMEM((N, C, ROWS), BF16),
            pltpu.VMEM((N, 8, ROWS), F32),
            pltpu.VMEM((N, C, ROWS), BF16),
            pltpu.VMEM((N, 8, ROWS), F32),
            dma((3,)),
            dma((6,)),
            dma((6,)),
            dma((7,)),
            dma((7,)),
            dma((N,)),
            dma((N,)),
            dma((N,)),
            dma((N,)),
            dma((GROUP,)),
            dma((GROUP,)),
            dma((GROUP,)),
            dma((GROUP,)),
            dma((N,)),
            dma((N,)),
            dma((N,)),
            dma((N,)),
        ],
        compiler_params=pltpu.CompilerParams(
            collective_id=0, has_side_effects=True, vmem_limit_bytes=50 << 20
        ),
        name="match_kernel",
    )(*(pltpu.with_memory_space_constraint(arg, pltpu.HBM) for arg in args))


def solution(mesh):
    in_specs = (P(("src", "tgt"), None), P("tgt", "src"), P())
    out_specs = (P(None, ("src", "tgt")), P(("src", "tgt"), None))
    return jax.shard_map(
        per_device, mesh=mesh, in_specs=in_specs, out_specs=out_specs, check_vma=False
    )
```

time: 43.3 us -> 39.5 us (0.912); the launches traced: 43.1 us -> 38.8 us
  local copies, waits for them, and re-layouts: 3.87 us -> 1.19 us
  Pallas kernels: 38.6 us -> 36.9 us
    unnamed x8 -> x2, local copies, waits for them, and re-layouts: 3.87 us -> 1.19 us
    pallas_call x1, Pallas kernels: 38.6 us -> 36.9 us  [per_device(): pl.pallas_call(kernel, out_shape=(jax.ShapeDtypeStruct((2, ROWS), F32), j...]
where the time goes in v3:
time: 39.5 us; the launch traced here: 38.8 us
  Pallas kernels  36.9 us (93%)
  local copies, waits for them, and re-layouts  1.19 us (3%)
  between operations  0.64 us (2%)
    pallas_call x1, Pallas kernels, per_device(): pl.pallas_call(kernel, out_shape=(jax.ShapeDtypeStruct((2, ROWS), F32), j...  36.9 us
    unnamed x2, local copies, waits for them, and re-layouts  1.19 us

profile of v3, /device:TPU:1, one launch (start us, length us, event | category | flops | bytes accessed | tf_op | source)
XLA Modules:
  0.0 38.8 jit_solution(8602341730064782867)
XLA Ops:
  0.6 36.9 %match_kernel.1 = (f32[2,128]{1,0:T(2,128)S(1)}, bf16[128,256]{1,0:T(8,128)(2,1)S(1)}) custom-call(bf16[128,256]{1,0:T(8,128)(2,1)} %src_hbm.1, bf16[64,1800]{1,0:T(8,128)(2,1)} %bitcast.1, bf16[256,256]{1,0:T(8,128)(2,1)} %proj_hbm.1), custom_call_target="tpu_custom_call" | custom-call | tf_op jit(solution)/shard_map/match_kernel/pallas_call | solution.py:336
  37.6 0.6 %copy.7 = f32[2,128]{1,0:T(2,128)} copy(f32[2,128]{1,0:T(2,128)S(1)} %get-tuple-element.4) | data formatting | bytes 2048
  38.2 0.6 %copy.8 = bf16[128,256]{1,0:T(8,128)(2,1)} copy(bf16[128,256]{1,0:T(8,128)(2,1)S(1)} %get-tuple-element.5) | data formatting | bytes 131072

commit v4 on v3

--- a/solution.py
+++ b/solution.py
@@ -23,6 +23,23 @@
 RING = ((1, 0, 0), (-1, 0, 1), (1, 0, 1), (-1, 0, 0), (1, -1, 0), (-1, 1, 1))
 
 
+ORDER = (
+    (2, 0), (1, 0), (2, 2), (2, 1), (2, 3), (1, 2), (3, 2), (1, 1),
+    (1, 3), (3, 1), (3, 3), (0, 2), (3, 0), (0, 1), (0, 3), (0, 0),
+)
+
+
+def table(which, half):
+    return sum(ORDER[8 * half + k][which] * 4**k for k in range(8))
+
+
+def offset(which, i):
+    if isinstance(i, int):
+        return jnp.int32(ORDER[i][which])
+    tab = jnp.where(i < 8, table(which, 0), table(which, 1))
+    return lax.shift_right_logical(tab, 2 * (i % 8)) % 4
+
+
 def place():
     s, t = lax.axis_index("src"), lax.axis_index("tgt")
     return (t // 4 % 2) * 2 + s // 2, t // 8, t % 4, s % 2
@@ -62,7 +79,8 @@
     qbuf,
     keys,
     keys_t,
-    scores,
+    scores_a,
+    scores_b,
     top_ref,
     stage,
     sstage,
@@ -110,15 +128,19 @@
         pltpu.make_async_copy(proj_hbm, proj_ref, in_sems.at[1]),
         pltpu.make_async_copy(src_hbm, src_ref, in_sems.at[2]),
     )
+    for load in loads:
+        load.start()
     barrier = pltpu.get_barrier_semaphore()
+    others = [(k, 0) for k in range(1, N)] + [(0, k) for k in range(1, N)]
     for other in (left, right, sibling):
         pl.semaphore_signal(barrier, inc=1, device_id=other, device_id_type=MESH)
-    for k in range(1, N):
-        pl.semaphore_signal(barrier, inc=1, device_id=peer(k, 0), device_id_type=MESH)
-        pl.semaphore_signal(barrier, inc=1, device_id=peer(0, k), device_id_type=MESH)
+    for da, db in others:
+        pl.semaphore_signal(barrier, inc=1, device_id=peer(da, db), device_id_type=MESH)
     for load in loads:
-        load.start()
-    pl.semaphore_wait(barrier, 3 + 2 * (N - 1))
+        load.wait()
+    queries = jnp.dot(src_ref[...], proj_ref[...], preferred_element_type=F32).astype(BF16)
+    qbuf[b * N + a] = (queries.astype(F32) * (1.0 / 16.0)).astype(BF16)
+    pl.semaphore_wait(barrier, 3 + len(others))
 
     def remote(src, dst, send_sem, recv_sem, other):
         return pltpu.make_async_remote_copy(
@@ -151,10 +173,11 @@
         ref = qbuf.at[b * N + (a + (N - k if arrival else 0)) % N]
         return remote(ref, ref, q1_send.at[k], q1_recv.at[k], peer(k, 0))
 
-    def q_row(k, arrival):
-        row = (b + (N - k if arrival else 0)) % N
-        ref = qbuf.at[pl.ds(row * N, N)]
-        return remote(ref, ref, q2_send.at[k], q2_recv.at[k], peer(0, k))
+    def q_cross(v, k, arrival):
+        row = (b + (N - v if arrival else 0)) % N
+        ref = qbuf.at[row * N + (a + N - k) % N]
+        i = v * N + k
+        return remote(ref, ref, q2_send.at[i], q2_recv.at[i], peer(0, v))
 
     def feat_copy(r, j):
         i = r * N + j
@@ -174,12 +197,14 @@
         ring_copy(k, False).start()
     core_copy(6, False).start()
 
-    for load in loads:
-        load.wait()
-    queries = jnp.dot(src_ref[...], proj_ref[...], preferred_element_type=F32).astype(BF16)
-    qbuf[b * N + a] = (queries.astype(F32) * (1.0 / 16.0)).astype(BF16)
-    for k in range(1, N):
+    for k in (1, 3, 2):
         q_block(k, False).start()
+
+    def pass_on(k):
+        for v in (2, 1, 3):
+            q_cross(v, k, False).start()
+
+    pass_on(0)
 
     mine = x // 2
     col = lax.broadcasted_iota(jnp.int32, (1, STRIP), 1)
@@ -204,14 +229,15 @@
             proj_ref[...], block, TN, preferred_element_type=F32
         ).astype(BF16)
 
+    for k in (1, 3):
+        q_block(k, True).wait_recv()
+        pass_on(k)
     for k in range(2):
         ring_copy(k, True).wait_recv()
         ring_copy(k + 4, False).start()
         core_copy(k, False).start()
-    for k in range(1, N):
-        q_block(k, True).wait_recv()
-    for k in (3, 2, 1):
-        q_row(k, False).start()
+    q_block(2, True).wait_recv()
+    pass_on(2)
     for k in range(2, 4):
         ring_copy(k, True).wait_recv()
         core_copy(k, False).start()
@@ -221,9 +247,6 @@
     for k in range(4, 6):
         ring_copy(k, True).wait_recv()
         core_copy(k, False).start()
-    for k in range(4, 6):
-        core_copy(k, True).wait_recv()
-    project(1)
 
     def relay(r):
         for j in range(1, N):
@@ -240,65 +263,121 @@
         relay_feat(r).start()
         relay_stat(r).start()
 
-    def turn(t, carry):
-        r = (t // 2 + 1) % N
-        js = (2 * (t % 2) + 1, (2 * (t % 2) + 2) % N)
-
-        @pl.when((t % 2 == 0) & (t < 6))
-        def _():
-            q_row(N - r, True).wait_recv()
-
-        def match(_, inner):
-            base = ((b + r) % N) * N
-            q = jnp.concatenate([qbuf[base + (a + j) % N] for j in js], axis=0)
-            tops = []
+    def apart(body):
+        def once(_, carry):
+            body()
+            return carry
+
+        lax.fori_loop(b, b + 1, once, 0)
+
+    def block(t, e):
+        i = 2 * t + e
+        return offset(0, i), offset(1, i)
+
+    def await_queries(t):
+        for e in range(2):
+            r, j = block(t, e)
+
+            @pl.when(r > 0)
+            def _():
+                q_cross(N - r, (N - j) % N, True).wait_recv()
+
+    def query_pair(t):
+        pair = []
+        for e in range(2):
+            r, j = block(t, e)
+            pair.append(qbuf[((b + r) % N) * N + (a + j) % N])
+        return jnp.concatenate(pair, axis=0)
+
+    def emit(t, o, m):
+        srow = lax.broadcasted_iota(jnp.int32, (8, 2 * ROWS), 0)
+        stat = jnp.where(srow == TOP, m, o[C : C + 8, :])
+        for e in range(2):
+            r, j = block(t, e)
+            lanes = slice(e * ROWS, (e + 1) * ROWS)
+            stage[r * N + j] = o[:C, lanes].astype(BF16)
+            sstage[r * N + j] = stat[:, lanes]
+
+            @pl.when(j > 0)
+            def _():
+                feat_copy(r, j).start()
+                stat_copy(r, j).start()
+
+    def step(t, slot, matching, gathering):
+        def body():
+            if matching:
+                q = query_pair(t + 1)
+            if gathering:
+                m = top_ref[slot]
+            tops, parts = [], []
             for e in range(2):
-                s = lax.dot_general(keys[e], q, NT, preferred_element_type=F32)
-                scores[e] = s
-                tops.append(jnp.max(s, axis=0, keepdims=True))
-            top_ref[...] = jnp.maximum(tops[0], tops[1])
-            return inner
-
-        def gather(_, inner):
-            m = top_ref[...]
-            o = jnp.zeros((C + AUG, 2 * ROWS), F32)
-            for e in range(2):
-                w = jnp.exp(scores[e] - m).astype(BF16)
-                o = o + jnp.dot(keys_t[e], w, preferred_element_type=F32)
-            srow = lax.broadcasted_iota(jnp.int32, (8, 2 * ROWS), 0)
-            stat = jnp.where(srow == TOP, m, o[C : C + 8, :])
-            for e, j in enumerate(js):
-                lanes = slice(e * ROWS, (e + 1) * ROWS)
-                stage[r * N + j] = o[:C, lanes].astype(BF16)
-                sstage[r * N + j] = stat[:, lanes]
-
-                @pl.when(j > 0)
-                def _():
-                    feat_copy(r, j).start()
-                    stat_copy(r, j).start()
-
-            return inner
-
-        lax.fori_loop(t, t + 1, match, 0)
-        lax.fori_loop(t, t + 1, gather, 0)
-
-        @pl.when((t % 2 == 1) & (t > 1))
-        def _():
-            relay((t - 1) // 2)
-
+                if matching:
+                    s = lax.dot_general(keys[e], q, NT, preferred_element_type=F32)
+                    (scores_b, scores_a)[slot][e] = s
+                    tops.append(jnp.max(s, axis=0, keepdims=True))
+                if gathering:
+                    w = jnp.exp((scores_a, scores_b)[slot][e] - m).astype(BF16)
+                    parts.append(jnp.dot(keys_t[e], w, preferred_element_type=F32))
+            if matching:
+                top_ref[1 - slot] = jnp.maximum(tops[0], tops[1])
+            if gathering:
+                emit(t, parts[0] + parts[1], m)
+
+        apart(body)
+
+    def first_match(e):
+        def body():
+            s = lax.dot_general(keys[e], query_pair(0), NT, preferred_element_type=F32)
+            scores_a[e] = s
+            top = jnp.max(s, axis=0, keepdims=True)
+            top_ref[0] = top if e == 0 else jnp.maximum(top_ref[0], top)
+
+        apart(body)
+
+    def two_turns(u, carry):
+        await_queries(2 * u + 1)
+        step(2 * u, 0, True, True)
+
+        await_queries(2 * u + 2)
+        step(2 * u + 1, 1, True, True)
         return carry
 
-    lax.fori_loop(0, 2 * N, turn, 0)
-
-    for j in range(1, N):
-        feat_copy(0, j).wait_recv()
-        stat_copy(0, j).wait_recv()
-    for r in range(1, N):
+    await_queries(0)
+    first_match(0)
+    for k in range(4, 6):
+        core_copy(k, True).wait_recv()
+    project(1)
+    first_match(1)
+    lax.fori_loop(0, N - 1, two_turns, 0)
+    relay(2)
+    await_queries(2 * N - 1)
+    step(2 * N - 2, 0, True, True)
+    step(2 * N - 1, 1, False, True)
+    relay(1)
+    relay(3)
+
+    def await_block(r, j):
+        feat_copy(r, j).wait_recv()
+        stat_copy(r, j).wait_recv()
+
+    def await_relay(r):
         relay_feat(r).wait_recv()
         relay_stat(r).wait_recv()
+
+    for j in (2, 1):
+        await_block(0, j)
+    await_relay(2)
+    top, feats, total = merge(
+        [stage[0], inbox[2], inbox[1], rin[2]],
+        [sstage[0], sinbox[2], sinbox[1], srin[2]],
+    )
+    trow = lax.broadcasted_iota(jnp.int32, (8, ROWS), 0)
+    await_block(0, 3)
+    for r in (1, 3):
+        await_relay(r)
     _, feats, total = merge(
-        [stage[0]] + [inbox[j] for j in range(1, N)] + [rin[r] for r in range(1, N)],
-        [sstage[0]] + [sinbox[j] for j in range(1, N)] + [srin[r] for r in range(1, N)],
+        [feats, inbox[3], rin[1], rin[3]],
+        [jnp.where(trow == TOP, top, total), sinbox[3], srin[1], srin[3]],
     )
     inv = 1.0 / total[0:1]
     s_idx, t_idx = lax.axis_index("src"), lax.axis_index("tgt")
@@ -316,17 +395,25 @@
         core_copy(k, False).wait_send()
     for k in range(1, N):
         q_block(k, False).wait_send()
-        q_row(k, False).wait_send()
-        relay_feat(k).wait_send()
-        relay_stat(k).wait_send()
+    for r in range(1, N):
+        relay_feat(r).wait_send()
+        relay_stat(r).wait_send()
 
     def settle(i, carry):
-        r, j = i // (N - 1), i % (N - 1) + 1
-        feat_copy(r, j).wait_send()
-        stat_copy(r, j).wait_send()
+        r, j = i // N, i % N
+
+        @pl.when(r > 0)
+        def _():
+            q_cross(r, j, False).wait_send()
+
+        @pl.when(j > 0)
+        def _():
+            feat_copy(r, j).wait_send()
+            stat_copy(r, j).wait_send()
+
         return carry
 
-    lax.fori_loop(0, N * (N - 1), settle, 0)
+    lax.fori_loop(0, GROUP, settle, 0)
 
 
 def per_device(source_feat, target_feat, proj):
@@ -349,7 +436,8 @@
             pltpu.VMEM((2, STRIP, C), BF16),
             pltpu.VMEM((2, C + AUG, STRIP), BF16),
             pltpu.VMEM((2, STRIP, 2 * ROWS), F32),
-            pltpu.VMEM((1, 2 * ROWS), F32),
+            pltpu.VMEM((2, STRIP, 2 * ROWS), F32),
+            pltpu.VMEM((2, 1, 2 * ROWS), F32),
             pltpu.VMEM((GROUP, C, ROWS), BF16),
             pltpu.VMEM((GROUP, 8, ROWS), F32),
             pltpu.VMEM((GROUP, C, ROWS), BF16),
@@ -365,8 +453,8 @@
             dma((7,)),
             dma((N,)),
             dma((N,)),
-            dma((N,)),
-            dma((N,)),
+            dma((GROUP,)),
+            dma((GROUP,)),
             dma((GROUP,)),
             dma((GROUP,)),
             dma((GROUP,)),

time: 39.5 us -> 38 us (0.962); the launches traced: 38.8 us -> 37.8 us
  Pallas kernels: 36.9 us -> 36 us
    pallas_call x1, Pallas kernels: 36.9 us -> 36 us  [per_device(): pl.pallas_call(kernel, out_shape=(jax.ShapeDtypeStruct((2, ROWS), F32), j...]
where the time goes in v4:
time: 38 us; the launch traced here: 37.8 us
  Pallas kernels  36 us (95%)
  local copies, waits for them, and re-layouts  1.19 us (3%)
  between operations  0.64 us (2%)
    pallas_call x1, Pallas kernels, per_device(): pl.pallas_call(kernel, out_shape=(jax.ShapeDtypeStruct((2, ROWS), F32), j...  36 us
    unnamed x2, local copies, waits for them, and re-layouts  1.19 us

profile of v4, /device:TPU:1, one launch (start us, length us, event | category | flops | bytes accessed | tf_op | source)
XLA Modules:
  0.0 37.8 jit_solution(17322981158930154601)
XLA Ops:
  0.6 36.0 %match_kernel.1 = (f32[2,128]{1,0:T(2,128)S(1)}, bf16[128,256]{1,0:T(8,128)(2,1)S(1)}) custom-call(bf16[128,256]{1,0:T(8,128)(2,1)} %src_hbm.1, bf16[64,1800]{1,0:T(8,128)(2,1)} %bitcast.1, bf16[256,256]{1,0:T(8,128)(2,1)} %proj_hbm.1), custom_call_target="tpu_custom_call" | custom-call | tf_op jit(solution)/shard_map/match_kernel/pallas_call | solution.py:423
  36.6 0.6 %copy.7 = f32[2,128]{1,0:T(2,128)} copy(f32[2,128]{1,0:T(2,128)S(1)} %get-tuple-element.4) | data formatting | bytes 2048
  37.2 0.6 %copy.8 = bf16[128,256]{1,0:T(8,128)(2,1)} copy(bf16[128,256]{1,0:T(8,128)(2,1)S(1)} %get-tuple-element.5) | data formatting | bytes 131072

commit v5 on v4

--- a/solution.py
+++ b/solution.py
@@ -14,6 +14,7 @@
 HCH = CROWS // 2
 N = 4
 GROUP = N * N
+PACKED = C + 32
 AUG = 16
 TOP = 4
 F32 = jnp.float32
@@ -54,7 +55,20 @@
     return pos - gy * W_GRID, gy
 
 
-def merge(feats, stats):
+def spread(stat):
+    high = stat.astype(BF16).astype(F32)
+    middle = (stat - high).astype(BF16).astype(F32)
+    parts = [high, middle, stat - high - middle, jnp.zeros_like(stat)]
+    return jnp.concatenate(parts, axis=0).astype(BF16)
+
+
+def whole(block):
+    parts = block[C:].astype(F32)
+    return block[:C], parts[0:8] + parts[8:16] + parts[16:24]
+
+
+def merge(blocks):
+    feats, stats = zip(*blocks)
     top = stats[0][TOP : TOP + 1]
     for stat in stats[1:]:
         top = jnp.maximum(top, stat[TOP : TOP + 1])
@@ -83,13 +97,9 @@
     scores_b,
     top_ref,
     stage,
-    sstage,
     inbox,
-    sinbox,
     rout,
-    srout,
     rin,
-    srin,
     in_sems,
     p_send,
     p_recv,
@@ -101,12 +111,8 @@
     q2_recv,
     o_send,
     o_recv,
-    t_send,
-    t_recv,
     ro_send,
     ro_recv,
-    rt_send,
-    rt_recv,
 ):
     x, y, z, c = place()
     a, b = z + c * (y - z), y + c * (z - y)
@@ -136,10 +142,6 @@
         pl.semaphore_signal(barrier, inc=1, device_id=other, device_id_type=MESH)
     for da, db in others:
         pl.semaphore_signal(barrier, inc=1, device_id=peer(da, db), device_id_type=MESH)
-    for load in loads:
-        load.wait()
-    queries = jnp.dot(src_ref[...], proj_ref[...], preferred_element_type=F32).astype(BF16)
-    qbuf[b * N + a] = (queries.astype(F32) * (1.0 / 16.0)).astype(BF16)
     pl.semaphore_wait(barrier, 3 + len(others))
 
     def remote(src, dst, send_sem, recv_sem, other):
@@ -183,20 +185,17 @@
         i = r * N + j
         return remote(stage.at[i], inbox.at[i], o_send.at[i], o_recv.at[i], peer(j, 0))
 
-    def stat_copy(r, j):
-        i = r * N + j
-        return remote(sstage.at[i], sinbox.at[i], t_send.at[i], t_recv.at[i], peer(j, 0))
-
     def relay_feat(r):
         return remote(rout.at[r], rin.at[r], ro_send.at[r], ro_recv.at[r], peer(0, r))
-
-    def relay_stat(r):
-        return remote(srout.at[r], srin.at[r], rt_send.at[r], rt_recv.at[r], peer(0, r))
 
     for k in range(4):
         ring_copy(k, False).start()
     core_copy(6, False).start()
 
+    for load in loads:
+        load.wait()
+    queries = jnp.dot(src_ref[...], proj_ref[...], preferred_element_type=F32).astype(BF16)
+    qbuf[b * N + a] = (queries.astype(F32) * (1.0 / 16.0)).astype(BF16)
     for k in (1, 3, 2):
         q_block(k, False).start()
 
@@ -251,17 +250,14 @@
     def relay(r):
         for j in range(1, N):
             feat_copy(r, j).wait_recv()
-            stat_copy(r, j).wait_recv()
         i = r * N
         top, feat, stat = merge(
-            [stage[i]] + [inbox[i + j] for j in range(1, N)],
-            [sstage[i]] + [sinbox[i + j] for j in range(1, N)],
+            [whole(stage[i])] + [whole(inbox[i + j]) for j in range(1, N)]
         )
         srow = lax.broadcasted_iota(jnp.int32, (8, ROWS), 0)
-        rout[r] = feat.astype(BF16)
-        srout[r] = jnp.where(srow == TOP, top, stat)
+        rout[r, 0:C] = feat.astype(BF16)
+        rout[r, C:PACKED] = spread(jnp.where(srow == TOP, top, stat))
         relay_feat(r).start()
-        relay_stat(r).start()
 
     def apart(body):
         def once(_, carry):
@@ -291,17 +287,16 @@
 
     def emit(t, o, m):
         srow = lax.broadcasted_iota(jnp.int32, (8, 2 * ROWS), 0)
-        stat = jnp.where(srow == TOP, m, o[C : C + 8, :])
+        stat = spread(jnp.where(srow == TOP, m, o[C : C + 8, :]))
         for e in range(2):
             r, j = block(t, e)
             lanes = slice(e * ROWS, (e + 1) * ROWS)
-            stage[r * N + j] = o[:C, lanes].astype(BF16)
-            sstage[r * N + j] = stat[:, lanes]
+            stage[r * N + j, 0:C] = o[:C, lanes].astype(BF16)
+            stage[r * N + j, C:PACKED] = stat[:, lanes]
 
             @pl.when(j > 0)
             def _():
                 feat_copy(r, j).start()
-                stat_copy(r, j).start()
 
     def step(t, slot, matching, gathering):
         def body():
@@ -358,26 +353,23 @@
 
     def await_block(r, j):
         feat_copy(r, j).wait_recv()
-        stat_copy(r, j).wait_recv()
 
     def await_relay(r):
         relay_feat(r).wait_recv()
-        relay_stat(r).wait_recv()
 
     for j in (2, 1):
         await_block(0, j)
     await_relay(2)
     top, feats, total = merge(
-        [stage[0], inbox[2], inbox[1], rin[2]],
-        [sstage[0], sinbox[2], sinbox[1], srin[2]],
+        [whole(stage[0]), whole(inbox[2]), whole(inbox[1]), whole(rin[2])]
     )
     trow = lax.broadcasted_iota(jnp.int32, (8, ROWS), 0)
     await_block(0, 3)
     for r in (1, 3):
         await_relay(r)
     _, feats, total = merge(
-        [feats, inbox[3], rin[1], rin[3]],
-        [jnp.where(trow == TOP, top, total), sinbox[3], srin[1], srin[3]],
+        [(feats, jnp.where(trow == TOP, top, total))]
+        + [whole(block) for block in (inbox[3], rin[1], rin[3])]
     )
     inv = 1.0 / total[0:1]
     s_idx, t_idx = lax.axis_index("src"), lax.axis_index("tgt")
@@ -397,7 +389,6 @@
         q_block(k, False).wait_send()
     for r in range(1, N):
         relay_feat(r).wait_send()
-        relay_stat(r).wait_send()
 
     def settle(i, carry):
         r, j = i // N, i % N
@@ -409,7 +400,6 @@
         @pl.when(j > 0)
         def _():
             feat_copy(r, j).wait_send()
-            stat_copy(r, j).wait_send()
 
         return carry
 
@@ -438,14 +428,10 @@
             pltpu.VMEM((2, STRIP, 2 * ROWS), F32),
             pltpu.VMEM((2, STRIP, 2 * ROWS), F32),
             pltpu.VMEM((2, 1, 2 * ROWS), F32),
-            pltpu.VMEM((GROUP, C, ROWS), BF16),
-            pltpu.VMEM((GROUP, 8, ROWS), F32),
-            pltpu.VMEM((GROUP, C, ROWS), BF16),
-            pltpu.VMEM((GROUP, 8, ROWS), F32),
-            pltpu.VMEM((N, C, ROWS), BF16),
-            pltpu.VMEM((N, 8, ROWS), F32),
-            pltpu.VMEM((N, C, ROWS), BF16),
-            pltpu.VMEM((N, 8, ROWS), F32),
+            pltpu.VMEM((GROUP, PACKED, ROWS), BF16),
+            pltpu.VMEM((GROUP, PACKED, ROWS), BF16),
+            pltpu.VMEM((N, PACKED, ROWS), BF16),
+            pltpu.VMEM((N, PACKED, ROWS), BF16),
             dma((3,)),
             dma((6,)),
             dma((6,)),
@@ -457,10 +443,6 @@
             dma((GROUP,)),
             dma((GROUP,)),
             dma((GROUP,)),
-            dma((GROUP,)),
-            dma((GROUP,)),
-            dma((N,)),
-            dma((N,)),
             dma((N,)),
             dma((N,)),
         ],

time: 38 us -> 37.7 us (level); the launches traced: 37.8 us -> 37.1 us
  Pallas kernels: 36 us -> 35.2 us
    pallas_call x1, Pallas kernels: 36 us -> 35.2 us  [per_device(): pl.pallas_call(kernel, out_shape=(jax.ShapeDtypeStruct((2, ROWS), F32), j...]
where the time goes in v5:
time: 37.7 us; the launch traced here: 37.1 us
  Pallas kernels  35.2 us (93%)
  local copies, waits for them, and re-layouts  1.19 us (3%)
  between operations  0.64 us (2%)
    pallas_call x1, Pallas kernels, per_device(): pl.pallas_call(kernel, out_shape=(jax.ShapeDtypeStruct((2, ROWS), F32), j...  35.2 us
    unnamed x2, local copies, waits for them, and re-layouts  1.19 us

profile of v5, /device:TPU:1, one launch (start us, length us, event | category | flops | bytes accessed | tf_op | source)
XLA Modules:
  0.0 37.1 jit_solution(15945888014364988933)
XLA Ops:
  0.6 35.2 %match_kernel.1 = (f32[2,128]{1,0:T(2,128)S(1)}, bf16[128,256]{1,0:T(8,128)(2,1)S(1)}) custom-call(bf16[128,256]{1,0:T(8,128)(2,1)} %src_hbm.1, bf16[64,1800]{1,0:T(8,128)(2,1)} %bitcast.1, bf16[256,256]{1,0:T(8,128)(2,1)} %proj_hbm.1), custom_call_target="tpu_custom_call" | custom-call | tf_op jit(solution)/shard_map/match_kernel/pallas_call | solution.py:413
  35.9 0.6 %copy.7 = f32[2,128]{1,0:T(2,128)} copy(f32[2,128]{1,0:T(2,128)S(1)} %get-tuple-element.4) | data formatting | bytes 2048
  36.4 0.6 %copy.8 = bf16[128,256]{1,0:T(8,128)(2,1)} copy(bf16[128,256]{1,0:T(8,128)(2,1)S(1)} %get-tuple-element.5) | data formatting | bytes 131072

commit v6 on v5

--- a/solution.py
+++ b/solution.py
@@ -224,6 +224,9 @@
     def project(e):
         block = chans[mine if e == 0 else 1 - mine]
         keys[e] = lax.dot_general(block, proj_ref[...], TN, preferred_element_type=F32).astype(BF16)
+
+    def project_turned(e):
+        block = chans[mine if e == 0 else 1 - mine]
         keys_t[e, 0:C, :] = lax.dot_general(
             proj_ref[...], block, TN, preferred_element_type=F32
         ).astype(BF16)
@@ -326,6 +329,7 @@
             scores_a[e] = s
             top = jnp.max(s, axis=0, keepdims=True)
             top_ref[0] = top if e == 0 else jnp.maximum(top_ref[0], top)
+            project_turned(e)
 
         apart(body)
 

time: 37.7 us -> 37.5 us (level); the launches traced: 37.1 us -> 37.4 us
  Pallas kernels: 35.2 us -> 35.6 us
where the time goes in v6:
time: 37.5 us; the launch traced here: 37.4 us
  Pallas kernels  35.6 us (95%)
  local copies, waits for them, and re-layouts  1.19 us (3%)
  between operations  0.64 us (2%)
    pallas_call x1, Pallas kernels, per_device(): pl.pallas_call(kernel, out_shape=(jax.ShapeDtypeStruct((2, ROWS), F32), j...  35.6 us
    unnamed x2, local copies, waits for them, and re-layouts  1.19 us

profile of v6, /device:TPU:1, one launch (start us, length us, event | category | flops | bytes accessed | tf_op | source)
XLA Modules:
  0.0 37.4 jit_solution(11536710958723836112)
XLA Ops:
  0.6 35.6 %match_kernel.1 = (f32[2,128]{1,0:T(2,128)S(1)}, bf16[128,256]{1,0:T(8,128)(2,1)S(1)}) custom-call(bf16[128,256]{1,0:T(8,128)(2,1)} %src_hbm.1, bf16[64,1800]{1,0:T(8,128)(2,1)} %bitcast.1, bf16[256,256]{1,0:T(8,128)(2,1)} %proj_hbm.1), custom_call_target="tpu_custom_call" | custom-call | tf_op jit(solution)/shard_map/match_kernel/pallas_call | solution.py:417
  36.2 0.6 %copy.7 = f32[2,128]{1,0:T(2,128)} copy(f32[2,128]{1,0:T(2,128)S(1)} %get-tuple-element.4) | data formatting | bytes 2048
  36.8 0.6 %copy.8 = bf16[128,256]{1,0:T(8,128)(2,1)} copy(bf16[128,256]{1,0:T(8,128)(2,1)S(1)} %get-tuple-element.5) | data formatting | bytes 131072
